TPU v7x, 1024 devices: a whole 8x8x8 slice. The times are simulated.
1024 devices in a mesh: dp: 128 (over y, z, core), tensor: 8 (over x).
Axes of the slice: x: 8, y: 8, z: 8, core: 2. Of those that a mesh axis runs over, the one named last changes fastest.
Arguments:
- activations: bfloat16 [32768, 3072], P('dp'), may hold values from -6 to 6
- basis_init: float32 [3, 1024, 64], P(None, 'tensor'), may hold values from -6 to 6
- owner_table: int32 [3], replicated, may hold values from 1 to 64, as said below
Outputs:
- covariance: float32 [3, 1024, 1024], P(None, 'tensor', 'dp')
- basis: float32 [3, 1024, 64], P(None, 'tensor')
- eigen: float32 [3, 64], replicated
- owned_eigen: float32 [256, 64], P('dp')
Inputs may be any that keep to these rules, and one draw needn't show every extreme that they name: `owner_table`: the owners are index 1 and index 64 of dp; one of them owns exactly 2 blocks, the other the rest.
All inputs are finite; a program needn't handle non-finite values.
Results may differ from a plain program's by a relative error of at most 0.0003.
Values sent between devices are 32-bit elements; how exact they have to be, the bound alone decides.
No kernel may reach another device: no remote copies, remote signals or barrier semaphores. Data moves between devices by JAX's collectives and lax.ppermute only.
A program may use at most 32 MiB of HBM per device.

v0:
```python
import math

import jax
import jax.numpy as jnp
from jax import lax
from jax.sharding import PartitionSpec as P

CAP = 2
ITERS = 2


def orthonormal(image, gram, valid):
    identity = jnp.eye(gram.shape[-1], dtype=jnp.float32)
    gram = jnp.where(valid[:, None, None], gram, identity)
    lower = jnp.linalg.cholesky(gram)
    current = lax.linalg.triangular_solve(
        lower, image, left_side=False, lower=True, transpose_a=True
    )
    return (current, jnp.diagonal(lower, axis1=1, axis2=2))


def body(activations, basis_init, owner_table):
    highest = lax.Precision.HIGHEST
    dp_count = lax.axis_size("dp")
    dp_index = lax.axis_index("dp")
    tp_index = lax.axis_index("tensor")
    tok_rows = activations.shape[0]
    blocks = basis_init.shape[0]
    slab_rows = basis_init.shape[1]
    order_size = activations.shape[1] // blocks
    total_tokens = tok_rows * dp_count
    blocked = activations.reshape(tok_rows, blocks, order_size)
    own_columns = lax.dynamic_slice_in_dim(blocked, tp_index * slab_rows, slab_rows, 2)
    cov_term = (
        jnp.einsum("tns,tnb->nsb", own_columns, blocked, preferred_element_type=jnp.float32)
        / total_tokens
    )
    summed = lax.psum_scatter(
        cov_term.reshape(blocks * slab_rows, order_size), "dp", scatter_dimension=1, tiled=True
    )
    col_count = summed.shape[1]
    cov_out = summed.reshape(blocks, slab_rows, col_count)
    positions = jnp.arange(blocks)
    earlier = (owner_table[:, None] == owner_table[None, :]) & (
        positions[None, :] < positions[:, None]
    )
    slot_of = jnp.sum(earlier.astype(jnp.int32), axis=1)
    table_match = (owner_table[None, :] == dp_index) & (
        slot_of[None, :] == jnp.arange(CAP)[:, None]
    )
    root_scale = math.sqrt(order_size)
    slot_count = CAP
    valid = jnp.any(table_match, axis=1)
    chosen = jnp.argmax(table_match.astype(jnp.int32), axis=1)
    shard_piece = lax.all_gather(summed, "dp", axis=1, tiled=True)
    piece_grid = shard_piece.reshape(blocks, slab_rows, shard_piece.shape[1])
    taken = jnp.where(valid[:, None, None], piece_grid[chosen], 0.0)
    current = jnp.where(valid[:, None, None], basis_init[chosen], 0.0)
    slot_values = jnp.zeros((slot_count, basis_init.shape[2]), jnp.float32)
    for iteration in range(ITERS):
        full_basis = lax.all_gather(current, "tensor", axis=1, tiled=True)
        image = jnp.einsum("wsb,wbk->wsk", taken, full_basis, precision=highest)
        gram = lax.psum(jnp.einsum("wsk,wsl->wkl", image, image, precision=highest), "tensor")
        current, slot_values = orthonormal(image, gram, valid)
    scaled = current * root_scale
    one_hot = ((chosen[:, None] == positions[None, :]) & valid[:, None]).astype(jnp.float32)
    basis_term = jnp.einsum("wb,wsk->bsk", one_hot, scaled, precision=highest)
    eigen_term = jnp.einsum("wb,wk->bk", one_hot, slot_values, precision=highest)
    basis, eigen = lax.psum((basis_term, eigen_term), "dp")
    owned_eigen = jnp.einsum("cb,bk->ck", table_match.astype(jnp.float32), eigen, precision=highest)
    return (cov_out, basis, eigen, owned_eigen)


def solution(mesh):
    return jax.shard_map(
        body,
        mesh=mesh,
        in_specs=(P("dp", None), P(None, "tensor", None), P()),
        out_specs=(P(None, "tensor", "dp"), P(None, "tensor", None), P(), P("dp", None)),
        check_vma=False,
    )
```

profile of v0, /device:TPU:1, one launch (start us, length us, event | category | flops | bytes accessed | tf_op | source)
XLA Modules:
  0.0 723.9 jit_solution(15443034037061200394)
XLA Ops:
  7.2 1.7 copy.63
  9.6 1.6 copy.65
  11.3 1.3 dynamic-slice
  13.2 224.1 %all-reduce.6.cloned.1.call-done = f32[384,1024]{0,1:T(8,128)} async-done(((f32[384,1024]{0,1:T(8,128)}), f32[384,1024]{0,1:T(8,128)}) %all-reduce.6.cloned.1.call-update) | async-done | bytes 1572880
  237.3 1.3 constant_dynamic-slice_fusion
  240.4 20.7 %all_gather.10 = f32[2,1024,64]{1,2,0:T(8,128)S(1)} all-gather(f32[2,128,64]{1,2,0:T(8,128)S(1)} %broadcast_select_fusion.2), channel_id=1, replica_groups=mesh['dp'=128,'tensor'=8] {'tensor'}, dimensions={1}, use_global_device_ids=true | all-gather | bytes 589824 | tf_op jit(solution)/shard_map/all_gather | solution.py:61
  261.1 1.3 fusion.44
  262.4 68.8 %all-gather.2.cloned.1.call-done = f32[384,1024]{0,1:T(8,128)} async-done(((f32[384,8]{0,1:T(8,128)}), f32[384,1024]{0,1:T(8,128)}) %all-gather.2.cloned.1.call-update) | async-done | bytes 1572880 | tf_op jit(solution)/shard_map/all_gather | solution.py:55
  331.2 1.9 copy.66
  333.7 1.4 fusion.3
  335.3 23.1 %psum.28 = f32[2,64,64]{1,2,0:T(8,128)S(1)} all-reduce(f32[2,64,64]{1,2,0:T(8,128)S(1)} %fusion.29), channel_id=1, replica_groups=mesh['dp'=128,'tensor'=8] {'tensor'}, use_global_device_ids=true, to_apply=%region_4.5 | all-reduce | flops 8192 | bytes 65536 | tf_op jit(solution)/shard_map/psum | solution.py:63
  358.6 11.7 %custom-call.10 = f32[2,64,64]{2,1,0:T(8,128)S(1)} custom-call(f32[2,64,64]{2,1,0:T(8,128)S(1)} %fusion.13), custom_call_target="Cholesky" | custom-call | tf_op jit(solution)/shard_map/jit(cholesky)/cholesky | solution.py:15
  370.6 9.8 %custom-call.11 = f32[2,1,64,64]{2,3,1,0:T(8,128)S(1)} custom-call(f32[2,1,64,64]{3,2,1,0:T(8,128)S(1)} %select_bitcast_fusion.1), custom_call_target="InvertDiagBlocksLowerTriangular" | custom-call | tf_op jit(solution)/shard_map/triangular_solve/custom-call.0 | solution.py:16
  380.7 19.4 %all_gather.11 = f32[2,1024,64]{1,2,0:T(8,128)S(1)} all-gather(f32[2,128,64]{1,2,0:T(8,128)S(1)} %convolution_bitcast_fusion.1), channel_id=1, replica_groups=mesh['dp'=128,'tensor'=8] {'tensor'}, dimensions={1}, use_global_device_ids=true | all-gather | bytes 589824 | tf_op jit(solution)/shard_map/all_gather | solution.py:61
  400.1 1.4 fusion.1
  401.7 21.7 %psum.29 = f32[2,64,64]{1,2,0:T(8,128)S(1)} all-reduce(f32[2,64,64]{1,2,0:T(8,128)S(1)} %fusion.30), channel_id=1, replica_groups=mesh['dp'=128,'tensor'=8] {'tensor'}, use_global_device_ids=true, to_apply=%region_7.10 | all-reduce | flops 8192 | bytes 65536 | tf_op jit(solution)/shard_map/psum | solution.py:63
  423.7 11.7 %custom-call.12 = f32[2,64,64]{2,1,0:T(8,128)S(1)} custom-call(f32[2,64,64]{2,1,0:T(8,128)S(1)} %fusion.11), custom_call_target="Cholesky" | custom-call | tf_op jit(solution)/shard_map/jit(cholesky)/cholesky | solution.py:15
  435.7 9.8 %custom-call.13 = f32[2,1,64,64]{2,3,1,0:T(8,128)S(1)} custom-call(f32[2,1,64,64]{3,2,1,0:T(8,128)S(1)} %get-tuple-element.32), custom_call_target="InvertDiagBlocksLowerTriangular" | custom-call | tf_op jit(solution)/shard_map/triangular_solve/custom-call.0 | solution.py:16
  445.8 1.0 fusion.14
  446.9 0.7 copy.74
  447.6 0.9 gather_fusion.2
  448.7 266.5 %psum.31 = f32[3,64]{1,0:T(4,128)S(1)} all-reduce(f32[3,64]{1,0:T(4,128)S(1)} %fusion.21), channel_id=1, replica_groups=mesh['dp'=128,'tensor'=8] {'dp'}, use_global_device_ids=true, to_apply=%region_9.12 | all-reduce | flops 192 | bytes 1536 | tf_op jit(solution)/shard_map/psum | solution.py:69
  715.2 0.7 fusion.31
  715.9 1.6 copy.75
  (44 shorter events, 5.3 us)
Async XLA Ops:
  7.2 232.5 %copy-start = (f32[3,128,64]{1,2,0:T(8,128)S(1)}, f32[3,128,64]{1,2,0:T(8,128)}, u32[]{:S(2)}) copy-start(f32[3,128,64]{1,2,0:T(8,128)} %param.7) | copy-start | bytes 294916
  7.2 230.1 %all-reduce.6.cloned.1.call-start = ((), (), s32[]{:S(2)}) async-start(), calls=%async_computation.2 | async-start | bytes 3145728
  11.2 227.5 %copy-start.2 = (s32[3]{0:T(128)S(1)}, s32[3]{0:T(128)}, u32[]{:S(2)}) copy-start(s32[3]{0:T(128)} %param.8) | copy-start | bytes 40
  11.2 319.9 %all-gather.2.cloned.1.call-start = ((), (), s32[]{:S(2)}) async-start(), calls=%async_computation | async-start | bytes 1585152 | tf_op jit(solution)/shard_map/all_gather | solution.py:55
  238.6 477.2 %all-reduce.4.cloned.1.call-start = ((), (), s32[]{:S(2)}) async-start(), calls=%async_computation.1 | async-start | bytes 262144 | tf_op jit(solution)/shard_map/psum | solution.py:69
  715.2 2.2 copy-start.1
Sparse Core Ops, SparseCore 0:
  11.4 225.8 all-reduce.5
  242.2 88.8 all-gather.1
  447.0 213.4 all-reduce.3
where the time goes:
time: 724 us
  blocking collectives  351 us (48%)
  waiting for transfers between devices  293 us (40%)
  other arithmetic  45 us (6%)
  between operations  14.6 us (2%)
  local copies, waits for them, and re-layouts  13.6 us (2%)
    psum x1, blocking collectives, body(): basis, eigen = lax.psum((basis_term, eigen_term), 'dp')  266 us
    unnamed x4, waiting for transfers between devices  224 us
    all_gather x1, waiting for transfers between devices, body(): shard_piece = lax.all_gather(summed, 'dp', axis=1, tiled=True)  68.8 us
    psum x2, blocking collectives, body(): lax.psum(jnp.einsum('wsk,wsl->wkl', image, image, precision=highest), 'te...  44.8 us
    all_gather x2, blocking collectives, body(): full_basis = lax.all_gather(current, 'tensor', axis=1, tiled=True)  40.1 us
    another operation x7, other arithmetic, orthonormal(): lower = jnp.linalg.cholesky(gram)  23.8 us
    another operation x5, other arithmetic, orthonormal(): lax.linalg.triangular_solve(lower, image, left_side=False, lower=True, tr...  19.8 us
  transfers between devices with their start and end apart: 3, of which 2 were waited for; matrix products, arithmetic and copies ran while one was open for 1% of the time, Pallas kernels for 0%

commit v1 on v0

v1 whole, which is shorter than its diff:
```python
import functools
import math

import jax
import jax.numpy as jnp
from jax import lax
from jax.experimental import pallas as pl
from jax.experimental.pallas import tpu as pltpu
from jax.sharding import PartitionSpec as P

CAP = 2
HIGHEST = lax.Precision.HIGHEST
SMALL = pltpu.CompilerParams(vmem_limit_bytes=16 << 20)


def product(a, b, contract_b):
    dims = (((1,), (contract_b,)), ((), ()))
    return lax.dot_general(a, b, dims, precision=HIGHEST, preferred_element_type=jnp.float32)


def product_rows(a, b):
    dims = (((0,), (0,)), ((), ()))
    return lax.dot_general(a, b, dims, precision=HIGHEST, preferred_element_type=jnp.float32)


def packed(gram):
    half = gram.shape[0] // 2
    return jnp.concatenate([gram[:half], gram[half:]], axis=1)


def unpacked(rows):
    half = rows.shape[1] // 2
    return jnp.concatenate([rows[:, :half], rows[:, half:]], axis=0)


def factor(grams):
    order = grams[0].shape[0]
    groups = order // 8
    sub = lax.broadcasted_iota(jnp.int32, (8, 2 * order), 0)
    row_at = lax.broadcasted_iota(jnp.int32, (order, order), 0)
    col_at = lax.broadcasted_iota(jnp.int32, (order, order), 1)
    identity = (row_at == col_at).astype(jnp.float32)
    tiles = []
    for gram in grams:
        both = jnp.concatenate([gram, identity], axis=1)
        tiles.append([both[8 * g : 8 * g + 8] for g in range(groups)])
    for pivot in range(order):
        group, place = divmod(pivot, 8)
        for held in tiles:
            row = held[group][place : place + 1]
            square = row[:, pivot : pivot + 1]
            inverse = lax.rsqrt(square)
            inverse = inverse * (1.5 - 0.5 * ((square * inverse) * inverse))
            row = row * inverse
            for g in range(group, groups):
                reduced = held[g] - (held[g][:, pivot : pivot + 1] * inverse) * row
                if g == group:
                    reduced = jnp.where(sub > place, reduced, jnp.where(sub == place, row, held[g]))
                held[g] = reduced
    results = []
    for held in tiles:
        both = jnp.concatenate(held, axis=0)
        diagonal = jnp.sum(both[:, :order] * identity, axis=0, keepdims=True)
        results.append((both[:, order:], diagonal))
    return results


def cov_kernel(scale, at_ref, slab_ref, columns_ref, keep_ref, send_ref):
    dims = (((0,), (0,)), ((), ()))
    term = lax.dot_general(columns_ref[...], slab_ref[...], dims, preferred_element_type=jnp.float32)
    pairs, _, share, rows = keep_ref.shape
    term = (term * scale).reshape(pairs, 2, share, rows)
    first = at_ref[1] == 0
    keep_ref[:, 0] = jnp.where(first, term[:, 0], term[:, 1])
    send_ref[:, 0] = jnp.where(first, term[:, 1], term[:, 0])


def piece_kernel(pieces_ref, basis_ref, own_ref, part_ref):
    blocks, share, _ = own_ref.shape
    vectors = basis_ref.shape[1]
    part_ref[...] = jnp.zeros(part_ref.shape, jnp.float32)
    for b in range(blocks):
        own = jnp.sum(pieces_ref[:, b], axis=0)
        own_ref[b] = own
        part_ref[:, b * vectors : (b + 1) * vectors] = product(own, basis_ref[b], 1)


def image_kernel(parts_ref, own_ref, out_ref):
    blocks = own_ref.shape[0]
    vectors = out_ref.shape[1] * 2 // 3
    images = parts_ref[0]
    for t in range(1, parts_ref.shape[0]):
        images = images + parts_ref[t]
    for b in range(blocks):
        image = images[:, b * vectors : (b + 1) * vectors]
        out_ref[b, :vectors] = product_rows(image, own_ref[b])
        out_ref[b, vectors:] = packed(product_rows(image, image))


def first_kernel(sums_ref, next_ref, gram_ref):
    blocks, vectors, _ = next_ref.shape
    factors = factor([unpacked(sums_ref[b, vectors:]) for b in range(blocks)])
    for b in range(blocks):
        image = product(factors[b][0], sums_ref[b, :vectors], 0)
        next_ref[b] = image
        gram_ref[b] = packed(product(image, image, 1))


def second_kernel(image_ref, grams_ref, basis_ref, eigen_ref):
    blocks = image_ref.shape[0]
    root_scale = math.sqrt(grams_ref.shape[0] * image_ref.shape[2])
    grams = []
    for b in range(blocks):
        gram = grams_ref[0, b]
        for t in range(1, grams_ref.shape[0]):
            gram = gram + grams_ref[t, b]
        grams.append(unpacked(gram))
    factors = factor(grams)
    for b in range(blocks):
        basis_ref[b] = product(factors[b][0], image_ref[b], 0) * root_scale
        eigen_ref[b : b + 1] = factors[b][1]


def copies(x, n):
    return jnp.broadcast_to(x[None], (n,) + x.shape)


def f32(*dims):
    return jax.ShapeDtypeStruct(dims, jnp.float32)


def body(activations, basis_init, owner_table):
    dp_count = lax.axis_size("dp")
    tp_count = lax.axis_size("tensor")
    dp_index = lax.axis_index("dp")
    tp_index = lax.axis_index("tensor")
    tok_rows = activations.shape[0]
    blocks, slab_rows, vectors = basis_init.shape
    order_size = activations.shape[1] // blocks
    share = order_size // dp_count
    pairs = dp_count // 2

    halves = pl.BlockSpec((pairs, 1, share, slab_rows), lambda b, at: (0, b, 0, 0))
    keep, send = pl.pallas_call(
        functools.partial(cov_kernel, 1.0 / (tok_rows * dp_count)),
        grid_spec=pltpu.PrefetchScalarGridSpec(
            num_scalar_prefetch=1,
            grid=(blocks,),
            in_specs=[
                pl.BlockSpec((tok_rows, slab_rows), lambda b, at: (0, b * tp_count + at[0])),
                pl.BlockSpec((tok_rows, order_size), lambda b, at: (0, b)),
            ],
            out_specs=(halves, halves),
        ),
        out_shape=(f32(pairs, blocks, share, slab_rows),) * 2,
        name="cov",
        compiler_params=SMALL,
    )(jnp.stack([tp_index, dp_index % 2]), activations, activations)
    partner = lax.ppermute(send, "dp", [(i, i ^ 1) for i in range(dp_count)])
    same_core = [list(range(core, dp_count, 2)) for core in range(2)]
    pieces = lax.all_to_all(keep + partner, "dp", 0, 0, axis_index_groups=same_core)
    lanes = -(-blocks * vectors // 128) * 128
    own, part = pl.pallas_call(
        piece_kernel, out_shape=(f32(blocks, share, slab_rows), f32(share, lanes)), name="piece", compiler_params=SMALL
    )(pieces, jnp.swapaxes(basis_init, 1, 2))

    parts = lax.all_to_all(copies(part, tp_count), "tensor", 0, 0)
    height = vectors + vectors // 2
    terms = pl.pallas_call(image_kernel, out_shape=f32(blocks, height, slab_rows), name="image", compiler_params=SMALL)(parts, own)
    rows = blocks * height
    each = -(-rows // dp_count)
    terms = terms.reshape(rows, slab_rows)
    terms = jnp.concatenate([terms, jnp.zeros((each * dp_count - rows, slab_rows), jnp.float32)], axis=0)
    terms = lax.all_to_all(terms.reshape(dp_count, each * slab_rows), "dp", 0, 0)
    terms = jnp.sum(terms, axis=0)
    sums = lax.all_to_all(copies(terms, dp_count), "dp", 0, 0)
    sums = sums.reshape(each * dp_count, slab_rows)[:rows].reshape(blocks, height, slab_rows)

    image, gram = pl.pallas_call(
        first_kernel, out_shape=(f32(blocks, vectors, slab_rows), f32(blocks, vectors // 2, 2 * vectors)), name="first", compiler_params=SMALL
    )(sums)
    grams = lax.all_to_all(copies(gram, tp_count), "tensor", 0, 0)
    basis, eigen = pl.pallas_call(
        second_kernel, out_shape=(f32(blocks, vectors, slab_rows), f32(blocks, vectors)), name="second", compiler_params=SMALL
    )(image, grams)

    positions = jnp.arange(blocks)
    earlier = (owner_table[:, None] == owner_table[None, :]) & (positions[None, :] < positions[:, None])
    slot_of = jnp.sum(earlier.astype(jnp.int32), axis=1)
    table_match = (owner_table[None, :] == dp_index) & (slot_of[None, :] == jnp.arange(CAP)[:, None])
    owned_eigen = jnp.sum(jnp.where(table_match[:, :, None], eigen[None], 0.0), axis=1)
    return (jnp.swapaxes(own, 1, 2), jnp.swapaxes(basis, 1, 2), eigen, owned_eigen)


def solution(mesh):
    return jax.shard_map(
        body,
        mesh=mesh,
        in_specs=(P("dp", None), P(None, "tensor", None), P()),
        out_specs=(P(None, "tensor", "dp"), P(None, "tensor", None), P(), P("dp", None)),
        check_vma=False,
    )
```

time: 724 us -> 148 us (0.20)
  waiting for transfers between devices: 293 us -> 15.4 us
  blocking collectives: 351 us -> 89.3 us
  other arithmetic: 45 us -> 1.95 us
  starting transfers between devices: 0.12 us -> 19.7 us
  Pallas kernels: 0 us -> 17.3 us
  between operations: 14.6 us -> 0.72 us
  local copies, waits for them, and re-layouts: 13.6 us -> 3.2 us
    psum x3 -> x0, blocking collectives: 311 us -> none  [the longest x1 266 us: body(): basis, eigen = lax.psum((basis_term, eigen_term), 'dp')]
    unnamed x4 -> x0, waiting for transfers between devices: 224 us -> none
    all_to_all x0 -> x4, blocking collectives: none -> 89.3 us  [the longest x1 31.9 us: body(): lax.all_to_all(keep + partner, 'dp', 0, 0, axis_index_groups=same_core)]
    all_gather x1 -> x0, waiting for transfers between devices: 68.8 us -> none  [body(): shard_piece = lax.all_gather(summed, 'dp', axis=1, tiled=True)]
    another operation x13 -> x1, other arithmetic: 44.2 us -> 0.08 us  [body(): jnp.stack([tp_index, dp_index % 2])]
    all_gather x2 -> x0, blocking collectives: 40.1 us -> none  [body(): full_basis = lax.all_gather(current, 'tensor', axis=1, tiled=True)]
    pallas_call x0 -> x5, Pallas kernels: none -> 17.3 us  [the longest x1 7.18 us: body(): pl.pallas_call(first_kernel, out_shape=(f32(blocks, vectors, slab_rows),...]
    ppermute x0 -> x1, starting transfers between devices: none -> 16 us  [body(): partner = lax.ppermute(send, 'dp', [(i, i ^ 1) for i in range(dp_count)])]
  transfers between devices with their start and end apart: 3 -> 2, of which waited for: 2 -> 2; matrix products, arithmetic and copies ran while one was open for 1% -> 0% of each run, Pallas kernels for 0% -> 0%
where the time goes in v1:
time: 148 us
  blocking collectives  89.3 us (60%)
  starting transfers between devices  19.7 us (13%)
  Pallas kernels  17.3 us (12%)
  waiting for transfers between devices  15.4 us (10%)
  local copies, waits for them, and re-layouts  3.2 us (2%)
  other arithmetic  1.95 us (1%)
    all_to_all x1, blocking collectives, body(): lax.all_to_all(keep + partner, 'dp', 0, 0, axis_index_groups=same_core)  31.9 us
    all_to_all x1, blocking collectives, body(): lax.all_to_all(terms.reshape(dp_count, each * slab_rows), 'dp', 0, 0)  24.7 us
    all_to_all x1, blocking collectives, body(): sums = lax.all_to_all(copies(terms, dp_count), 'dp', 0, 0)  19.3 us
    ppermute x1, starting transfers between devices, body(): partner = lax.ppermute(send, 'dp', [(i, i ^ 1) for i in range(dp_count)])  16 us
    all_to_all x1, blocking collectives, body(): parts = lax.all_to_all(copies(part, tp_count), 'tensor', 0, 0)  13.5 us
    all_to_all x1, waiting for transfers between devices, body(): grams = lax.all_to_all(copies(gram, tp_count), 'tensor', 0, 0)  13.5 us
    pallas_call x1, Pallas kernels, body(): pl.pallas_call(first_kernel, out_shape=(f32(blocks, vectors, slab_rows),...  7.18 us
    pallas_call x1, Pallas kernels, body(): pl.pallas_call(second_kernel, out_shape=(f32(blocks, vectors, slab_rows),...  6.94 us
  transfers between devices with their start and end apart: 2, of which 2 were waited for; matrix products, arithmetic and copies ran while one was open for 0% of the time, Pallas kernels for 0%

profile of v1, /device:TPU:1, one launch (start us, length us, event | category | flops | bytes accessed | tf_op | source)
XLA Modules:
  0.0 147.5 jit_solution(7048936181694465931)
XLA Ops:
  0.6 0.1 pad_add_fusion.at_ref
  0.7 1.4 copy-done
  2.1 2.0 %cov.1 = (f32[64,3,8,128]{3,2,1,0:T(8,128)S(1)}, f32[64,3,8,128]{3,2,1,0:T(8,128)S(1)}) custom-call(s32[2]{0:T(128)S(1)} %pad_add_fusion.at_ref, bf16[256,3072]{1,0:T(8,128)(2,1)S(1)} %copy-done, bf16[256,3072]{1,0:T(8,128)(2,1)S(1)} %copy-done), custom_call_target="tpu_custom_call" | custom-call | tf_op jit(solution)/shard_map/cov/pallas_call | solution.py:144
  4.1 16.0 %collective-permute-start = (f32[64,3,8,128]{3,2,1,0:T(8,128)S(1)}, f32[64,3,8,128]{3,2,1,0:T(8,128)S(1)}, u32[]{:S(2)}, u32[]{:S(2)}) collective-permute-start(f32[64,3,8,128]{3,2,1,0:T(8,128)S(1)} %get-tuple-element.13), channel_id=1, source_target_pairs={{0,8},{8,0},{16,24},{24,16},{32,40},{40,32},{48,56},{56,48},{64,72... | collective-permute-start | bytes 2359304 | tf_op jit(solution)/shard_map/ppermute | solution.py:159
  20.1 1.9 %collective-permute-done = f32[64,3,8,128]{3,2,1,0:T(8,128)S(1)} collective-permute-done((f32[64,3,8,128]{3,2,1,0:T(8,128)S(1)}, f32[64,3,8,128]{3,2,1,0:T(8,128)S(1)}, u32[]{:S(2)}, u32[]{:S(2)}) %collective-permute-start) | collective-permute-done | bytes 786464 | tf_op jit(solution)/shard_map/ppermute | solution.py:159
  22.0 0.1 add.10
  22.2 31.9 %all_to_all.30.pieces_ref = f32[64,3,8,128]{3,2,1,0:T(8,128)S(1)} all-to-all(f32[64,3,8,128]{3,2,1,0:T(8,128)S(1)} %add.10), channel_id=1, replica_groups={{0,16,32,48,64,80,96,112,128,144,160,176,192,208,224,240,256,272,288,30..., dimensions={0} | all-to-all | bytes 1572864 | tf_op jit(solution)/shard_map/all_to_all | solution.py:161
  54.0 0.7 piece.1
  54.7 13.5 %all_to_all.31.parts_ref = f32[8,8,256]{2,1,0:T(8,128)S(1)} all-to-all(f32[8,8,256]{2,1,0:T(8,128)S(1)} %broadcast_in_dim.19), channel_id=1, replica_groups=mesh['dp'=128,'tensor'=8] {'tensor'}, dimensions={0} | all-to-all | bytes 131072 | tf_op jit(solution)/shard_map/all_to_all | solution.py:167
  68.2 0.7 copy-done.2
  68.9 0.5 image.1
  69.4 24.7 %all_to_all.32 = f32[128,1,384]{2,1,0:T(1,128)S(1)} all-to-all(f32[128,1,384]{2,1,0:T(1,128)S(1)} %bitcast.12), channel_id=1, replica_groups=mesh['dp'=128,'tensor'=8] {'dp'}, dimensions={0} | all-to-all | bytes 393216 | tf_op jit(solution)/shard_map/all_to_all | solution.py:174
  94.1 0.2 reduce_sum.27
  94.3 0.1 broadcast_in_dim.20
  94.4 19.3 %all_to_all.33 = f32[128,1,384]{2,1,0:T(1,128)S(1)} all-to-all(f32[128,1,384]{2,1,0:T(1,128)S(1)} %broadcast_in_dim.20), channel_id=1, replica_groups=mesh['dp'=128,'tensor'=8] {'dp'}, dimensions={0} | all-to-all | bytes 393216 | tf_op jit(solution)/shard_map/all_to_all | solution.py:176
  113.7 0.1 slice.6
  113.8 7.2 %first.1 = (f32[3,64,128]{2,1,0:T(8,128)S(1)}, f32[3,32,128]{2,1,0:T(8,128)S(1)}) custom-call(f32[3,96,128]{2,1,0:T(8,128)S(1)} %bitcast.8), custom_call_target="tpu_custom_call" | custom-call | tf_op jit(solution)/shard_map/first/pallas_call | solution.py:179
  121.0 0.9 broadcast_in_dim.21
  121.8 3.6 %all-to-all-start.4 = ((f32[8,3,32,128]{3,2,1,0:T(8,128)}), f32[8,3,32,128]{3,2,1,0:T(8,128)S(1)}, u32[]{:S(2)}, u32[]{:S(2)}) async-start(f32[8,3,32,128]{3,2,1,0:T(8,128)} %broadcast_in_dim.21), calls=%async_computation.4 | async-start | bytes 786432 | tf_op jit(solution)/shard_map/all_to_all | solution.py:182
  125.5 0.2 convert_reduce_fusion
  125.7 0.1 fusion.1
  125.7 13.5 %all-to-all-done.4.grams_ref = f32[8,3,32,128]{3,2,1,0:T(8,128)S(1)} async-done(((f32[8,3,32,128]{3,2,1,0:T(8,128)}), f32[8,3,32,128]{3,2,1,0:T(8,128)S(1)}, u32[]{:S(2)}, u32[]{:S(2)}) %all-to-all-start.4) | async-done | bytes 393248 | tf_op jit(solution)/shard_map/all_to_all | solution.py:182
  139.2 6.9 %second.1 = (f32[3,64,128]{2,1,0:T(8,128)}, f32[3,64]{1,0:T(4,128)}) custom-call(f32[3,64,128]{2,1,0:T(8,128)S(1)} %get-tuple-element.16.image_ref, f32[8,3,32,128]{3,2,1,0:T(8,128)S(1)} %all-to-all-done.4.grams_ref), custom_call_target="tpu_custom_call" | custom-call | tf_op jit(solution)/shard_map/second/pallas_call | solution.py:183
  146.2 1.3 select_reduce_fusion
  (9 shorter events, 0.0 us)
Async XLA Ops:
  0.7 1.4 copy-start
  4.1 17.9 %collective-permute-start = (f32[64,3,8,128]{3,2,1,0:T(8,128)S(1)}, f32[64,3,8,128]{3,2,1,0:T(8,128)S(1)}, u32[]{:S(2)}, u32[]{:S(2)}) collective-permute-start(f32[64,3,8,128]{3,2,1,0:T(8,128)S(1)} %get-tuple-element.13), channel_id=1, source_target_pairs={{0,8},{8,0},{16,24},{24,16},{32,40},{40,32},{48,56},{56,48},{64,72... | collective-permute-start | bytes 2359304 | tf_op jit(solution)/shard_map/ppermute | solution.py:159
  22.0 32.0 %copy-start.1 = (f32[3,128,64]{1,2,0:T(8,128)S(1)}, f32[3,128,64]{1,2,0:T(8,128)}, u32[]{:S(2)}) copy-start(f32[3,128,64]{1,2,0:T(8,128)} %param.4) | copy-start | bytes 294916
  68.2 0.7 copy-start.2
  69.4 56.1 %copy-start.3 = (s32[3]{0:T(128)S(1)}, s32[3]{0:T(128)}, u32[]{:S(2)}) copy-start(s32[3]{0:T(128)} %param.5) | copy-start | bytes 40
  121.8 17.4 %all-to-all-start.4 = ((f32[8,3,32,128]{3,2,1,0:T(8,128)}), f32[8,3,32,128]{3,2,1,0:T(8,128)S(1)}, u32[]{:S(2)}, u32[]{:S(2)}) async-start(f32[8,3,32,128]{3,2,1,0:T(8,128)} %broadcast_in_dim.21), calls=%async_computation.4 | async-start | bytes 786432 | tf_op jit(solution)/shard_map/all_to_all | solution.py:182

commit v2 on v1

v2 whole, which is shorter than its diff:
```python
import functools
import math

import jax
import jax.numpy as jnp
from jax import lax
from jax.experimental import pallas as pl
from jax.experimental.pallas import tpu as pltpu
from jax.sharding import PartitionSpec as P

CAP = 2
HIGHEST = lax.Precision.HIGHEST
SMALL = pltpu.CompilerParams(vmem_limit_bytes=16 << 20)


def product(a, b, contract_b):
    dims = (((1,), (contract_b,)), ((), ()))
    return lax.dot_general(a, b, dims, precision=HIGHEST, preferred_element_type=jnp.float32)


def product_rows(a, b):
    dims = (((0,), (0,)), ((), ()))
    return lax.dot_general(a, b, dims, precision=HIGHEST, preferred_element_type=jnp.float32)


def packed(gram):
    half = gram.shape[0] // 2
    return jnp.concatenate([gram[:half], gram[half:]], axis=1)


def unpacked(rows):
    half = rows.shape[1] // 2
    return jnp.concatenate([rows[:, :half], rows[:, half:]], axis=0)


def quadrants(gram):
    half = gram.shape[0] // 2
    quads = (gram[:half, :half], gram[half:, :half], gram[half:, half:])
    return jnp.concatenate([jnp.concatenate([q[r : r + 8] for r in range(0, half, 8)], axis=1) for q in quads], axis=0)


def whole_gram(rows, order):
    half = order // 2
    quads = []
    for q in range(3):
        part = rows[q * 8 : q * 8 + 8]
        quads.append(jnp.concatenate([part[:, c : c + half] for c in range(0, part.shape[1], half)], axis=0))
    upper = jnp.concatenate([quads[0], quads[1].T], axis=1)
    lower = jnp.concatenate([quads[1], quads[2]], axis=1)
    return jnp.concatenate([upper, lower], axis=0)


def refined_rsqrt(x):
    r = lax.rsqrt(x)
    return r * (1.5 - 0.5 * ((x * r) * r))


def factor(grams):
    order = grams[0].shape[0]
    groups = order // 8
    wide = 2 * order
    sub = lax.broadcasted_iota(jnp.int32, (8, wide), 0)
    lane = lax.broadcasted_iota(jnp.int32, (8, wide), 1)
    row_at = lax.broadcasted_iota(jnp.int32, (order, order), 0)
    col_at = lax.broadcasted_iota(jnp.int32, (order, order), 1)
    identity = (row_at == col_at).astype(jnp.float32)

    def full(x):
        return jnp.broadcast_to(x, (8, wide))

    tiles = []
    for gram in grams:
        both = jnp.concatenate([gram, identity], axis=1)
        tiles.append([both[8 * g : 8 * g + 8] for g in range(groups)])
    for pivot in range(order):
        group, place = divmod(pivot, 8)
        for held in tiles:
            own = full(held[group][:, pivot : pivot + 1])
            scaled = full(held[group][place : place + 1]) * (1.0 / full(own[place : place + 1]))
            for g in range(group, groups):
                if g == group and place == 7:
                    continue
                column = own if g == group else full(held[g][:, pivot : pivot + 1])
                reduced = held[g] - column * scaled
                held[g] = jnp.where(sub > place, reduced, held[g]) if g == group else reduced
    results = []
    for held in tiles:
        rows = []
        for g in range(groups):
            square = jnp.sum(jnp.where(lane == sub + 8 * g, held[g], 0.0), axis=1, keepdims=True)
            rows.append(held[g] * refined_rsqrt(square))
        both = jnp.concatenate(rows, axis=0)
        results.append((both[:, order:], jnp.sum(both[:, :order] * identity, axis=0, keepdims=True)))
    return results


def cov_kernel(scale, at_ref, core_ref, slab_ref, columns_ref, keep_ref, send_ref):
    dims = (((0,), (0,)), ((), ()))
    term = lax.dot_general(columns_ref[...], slab_ref[...], dims, preferred_element_type=jnp.float32)
    pairs, _, share, rows = keep_ref.shape
    term = (term * scale).reshape(pairs, 2, share, rows)
    first = core_ref[0] == 0
    keep_ref[:, 0] = jnp.where(first, term[:, 0], term[:, 1])
    send_ref[:, 0] = jnp.where(first, term[:, 1], term[:, 0])


def piece_kernel(pieces_ref, basis_ref, out_ref, own_ref, part_ref):
    blocks, share, _ = own_ref.shape
    vectors = basis_ref.shape[1]
    part_ref[...] = jnp.zeros(part_ref.shape, jnp.float32)
    for b in range(blocks):
        own = jnp.sum(pieces_ref[:, b], axis=0)
        out_ref[b] = own
        own_ref[b] = own
        part_ref[:, b * vectors : (b + 1) * vectors] = product(own, basis_ref[b], 1)


def image_kernel(vectors, parts_ref, own_ref, out_ref):
    blocks = own_ref.shape[0]
    height = vectors + vectors // 2
    images = parts_ref[0]
    for t in range(1, parts_ref.shape[0]):
        images = images + parts_ref[t]
    for b in range(blocks):
        image = images[:, b * vectors : (b + 1) * vectors]
        out_ref[b * height : b * height + vectors] = product_rows(image, own_ref[b])
        out_ref[b * height + vectors : (b + 1) * height] = packed(product_rows(image, image))
    rest = out_ref.shape[0] - blocks * height
    if rest > 0:
        out_ref[blocks * height :] = jnp.zeros((rest, out_ref.shape[1]), jnp.float32)


def first_kernel(sums_ref, next_ref, gram_ref):
    blocks, vectors, _ = next_ref.shape
    height = vectors + vectors // 2
    grams = [unpacked(sums_ref[b * height + vectors : (b + 1) * height]) for b in range(blocks)]
    factors = factor(grams)
    for b in range(blocks):
        image = product(factors[b][0], sums_ref[b * height : b * height + vectors], 0)
        next_ref[b] = image
        gram_ref[b] = quadrants(product(image, image, 1))


def second_kernel(owner_ref, index_ref, image_ref, grams_ref, basis_ref, eigen_ref, owned_ref):
    blocks, vectors, slab_rows = image_ref.shape
    root_scale = math.sqrt(grams_ref.shape[0] * slab_rows)
    grams = []
    for b in range(blocks):
        rows = grams_ref[0, b]
        for t in range(1, grams_ref.shape[0]):
            rows = rows + grams_ref[t, b]
        grams.append(whole_gram(rows, vectors))
    factors = factor(grams)
    owned = [jnp.zeros((1, vectors), jnp.float32) for _ in range(CAP)]
    for b in range(blocks):
        basis_ref[b] = product(factors[b][0], image_ref[b], 0) * root_scale
        eigen_ref[b : b + 1] = factors[b][1]
        slot = jnp.int32(0)
        for earlier in range(b):
            slot = slot + jnp.where(owner_ref[earlier] == owner_ref[b], 1, 0)
        mine = owner_ref[b] == index_ref[0]
        for s in range(CAP):
            owned[s] = owned[s] + jnp.where(mine & (slot == s), factors[b][1], 0.0)
    for s in range(CAP):
        owned_ref[s : s + 1] = owned[s]


def copies(x, n):
    return jnp.broadcast_to(x[None], (n,) + x.shape)


def f32(*dims):
    return jax.ShapeDtypeStruct(dims, jnp.float32)


def body(activations, basis_init, owner_table):
    dp_count = lax.axis_size("dp")
    tp_count = lax.axis_size("tensor")
    dp_index = lax.axis_index("dp")
    tp_index = lax.axis_index("tensor")
    tok_rows = activations.shape[0]
    blocks, slab_rows, vectors = basis_init.shape
    order_size = activations.shape[1] // blocks
    share = order_size // dp_count
    pairs = dp_count // 2

    halves = pl.BlockSpec((pairs, 1, share, slab_rows), lambda b, at, core: (0, b, 0, 0))
    keep, send = pl.pallas_call(
        functools.partial(cov_kernel, 1.0 / (tok_rows * dp_count)),
        grid_spec=pltpu.PrefetchScalarGridSpec(
            num_scalar_prefetch=2,
            grid=(blocks,),
            in_specs=[
                pl.BlockSpec((tok_rows, slab_rows), lambda b, at, core: (0, b * tp_count + at[0])),
                pl.BlockSpec((tok_rows, order_size), lambda b, at, core: (0, b)),
            ],
            out_specs=(halves, halves),
        ),
        out_shape=(f32(pairs, blocks, share, slab_rows),) * 2,
        name="cov",
        compiler_params=SMALL,
    )(jnp.reshape(tp_index, (1,)), jnp.reshape(dp_index & 1, (1,)), activations, activations)
    other_core = [(i, i ^ 1) for i in range(dp_count)]
    partner = lax.ppermute(send, "dp", other_core)
    same_core = [list(range(core, dp_count, 2)) for core in range(2)]
    pieces = lax.all_to_all(keep + partner, "dp", 0, 0, axis_index_groups=same_core)
    lanes = -(-blocks * vectors // 128) * 128
    piece = f32(blocks, share, slab_rows)
    cov_out, own, part = pl.pallas_call(
        piece_kernel, out_shape=(piece, piece, f32(share, lanes)), name="piece", compiler_params=SMALL
    )(pieces, jnp.swapaxes(basis_init, 1, 2))

    parts = lax.all_to_all(copies(part, tp_count), "tensor", 0, 0)
    height = vectors + vectors // 2
    each = -(-blocks * height // pairs)
    terms = pl.pallas_call(
        functools.partial(image_kernel, vectors), out_shape=f32(each * pairs, slab_rows), name="image", compiler_params=SMALL
    )(parts, own)
    terms = lax.all_to_all(terms.reshape(pairs, each * slab_rows), "dp", 0, 0, axis_index_groups=same_core)
    terms = jnp.sum(terms, axis=0)
    terms = terms + lax.ppermute(terms, "dp", other_core)
    sums = lax.all_to_all(copies(terms, pairs), "dp", 0, 0, axis_index_groups=same_core)
    sums = sums.reshape(each * pairs, slab_rows)

    image, gram = pl.pallas_call(
        first_kernel, out_shape=(f32(blocks, vectors, slab_rows), f32(blocks, 24, 128)), name="first", compiler_params=SMALL
    )(sums)
    grams = lax.all_to_all(copies(gram, tp_count), "tensor", 0, 0)
    scalars = pl.BlockSpec(memory_space=pltpu.SMEM)
    whole = pl.BlockSpec(memory_space=pltpu.VMEM)
    basis, eigen, owned = pl.pallas_call(
        second_kernel,
        in_specs=[scalars, scalars, whole, whole],
        out_shape=(f32(blocks, vectors, slab_rows), f32(blocks, vectors), f32(CAP, vectors)),
        name="second",
        compiler_params=SMALL,
    )(owner_table, jnp.reshape(dp_index, (1,)), image, grams)
    return (jnp.swapaxes(cov_out, 1, 2), jnp.swapaxes(basis, 1, 2), eigen, owned)


def solution(mesh):
    return jax.shard_map(
        body,
        mesh=mesh,
        in_specs=(P("dp", None), P(None, "tensor", None), P()),
        out_specs=(P(None, "tensor", "dp"), P(None, "tensor", None), P(), P("dp", None)),
        check_vma=False,
    )
```

time: 148 us -> 144 us (0.973)
  waiting for transfers between devices: 15.4 us -> 2.69 us
  Pallas kernels: 17.3 us -> 22.2 us
  blocking collectives: 89.3 us -> 93.4 us
  starting transfers between devices: 19.7 us -> 21.6 us
  other arithmetic: 1.95 us -> 0.23 us
  local copies, waits for them, and re-layouts: 3.2 us -> 1.54 us
    all_to_all x1 -> x0, waiting for transfers between devices: 13.5 us -> none  [body(): grams = lax.all_to_all(copies(gram, tp_count), 'tensor', 0, 0)]
    ppermute x1 -> x2, starting transfers between devices: 16 us -> 21.6 us  [the longest x1 16 us: body(): partner = lax.ppermute(send, 'dp', other_core)]
    all_to_all x2 -> x3, blocking collectives: 44 us -> 48 us  [the longest x1 20.2 us: body(): lax.all_to_all(terms.reshape(pairs, each * slab_rows), 'dp', 0, 0, axis_i...]
    all_to_all x1 -> x0, starting transfers between devices: 3.63 us -> none  [body(): grams = lax.all_to_all(copies(gram, tp_count), 'tensor', 0, 0)]
    pallas_call x3, Pallas kernels: 8.1 us -> 11.3 us  [the longest x1 10.2 us: body(): pl.pallas_call(second_kernel, in_specs=[scalars, scalars, whole, whole],...]
    pallas_call x1, Pallas kernels: 7.18 us -> 9.45 us  [body(): pl.pallas_call(first_kernel, out_shape=(f32(blocks, vectors, slab_rows),...]
    reduce_sum x2 -> x0, other arithmetic: 1.51 us -> none  [the longest x1 1.32 us: body(): jnp.sum(jnp.where(table_match[:, :, None], eigen[None], 0.0), axis=1)]
where the time goes in v2:
time: 144 us; the launch traced here: 142 us
  blocking collectives  93.4 us (65%)
  Pallas kernels  22.2 us (15%)
  starting transfers between devices  21.6 us (15%)
  waiting for transfers between devices  2.69 us (2%)
  local copies, waits for them, and re-layouts  1.54 us (1%)
    all_to_all x1, blocking collectives, body(): lax.all_to_all(keep + partner, 'dp', 0, 0, axis_index_groups=same_core)  31.9 us
    all_to_all x1, blocking collectives, body(): lax.all_to_all(terms.reshape(pairs, each * slab_rows), 'dp', 0, 0, axis_i...  20.2 us
    ppermute x1, starting transfers between devices, body(): partner = lax.ppermute(send, 'dp', other_core)  16 us
    all_to_all x1, blocking collectives, body(): lax.all_to_all(copies(terms, pairs), 'dp', 0, 0, axis_index_groups=same_c...  15.7 us
    all_to_all x1, blocking collectives, body(): parts = lax.all_to_all(copies(part, tp_count), 'tensor', 0, 0)  13.5 us
    all_to_all x1, blocking collectives, body(): grams = lax.all_to_all(copies(gram, tp_count), 'tensor', 0, 0)  12.2 us
    pallas_call x1, Pallas kernels, body(): pl.pallas_call(second_kernel, in_specs=[scalars, scalars, whole, whole],...  10.2 us
    pallas_call x1, Pallas kernels, body(): pl.pallas_call(first_kernel, out_shape=(f32(blocks, vectors, slab_rows),...  9.45 us
  transfers between devices with their start and end apart: 2, of which 2 were waited for; matrix products, arithmetic and copies ran while one was open for 0% of the time, Pallas kernels for 0%

profile of v2, /device:TPU:1, one launch (start us, length us, event | category | flops | bytes accessed | tf_op | source)
XLA Modules:
  0.0 142.3 jit_solution(1422390300009831552)
XLA Ops:
  0.6 0.0 copy-start
  0.6 1.4 copy-done
  2.0 1.4 %cov.1 = (f32[64,3,8,128]{3,2,1,0:T(8,128)S(1)}, f32[64,3,8,128]{3,2,1,0:T(8,128)S(1)}) custom-call(s32[1]{0:T(128)} %bitcast.at_ref, s32[1]{0:T(128)} %bitcast.1.core_ref, bf16[256,3072]{1,0:T(8,128)(2,1)S(1)} %copy-done, bf16[256,3072]{1,0:T(8,128)(2,1)S(1)} %copy-done), custom_call_target="tpu_custom_call" | custom-call | tf_op jit(solution)/shard_map/cov/pallas_call | solution.py:188
  3.5 16.0 %collective-permute-start = (f32[64,3,8,128]{3,2,1,0:T(8,128)S(1)}, f32[64,3,8,128]{3,2,1,0:T(8,128)S(1)}, u32[]{:S(2)}, u32[]{:S(2)}) collective-permute-start(f32[64,3,8,128]{3,2,1,0:T(8,128)S(1)} %get-tuple-element.15), channel_id=1, source_target_pairs={{0,8},{8,0},{16,24},{24,16},{32,40},{40,32},{48,56},{56,48},{64,72... | collective-permute-start | bytes 2359304 | tf_op jit(solution)/shard_map/ppermute | solution.py:204
  19.5 1.9 %collective-permute-done = f32[64,3,8,128]{3,2,1,0:T(8,128)S(1)} collective-permute-done((f32[64,3,8,128]{3,2,1,0:T(8,128)S(1)}, f32[64,3,8,128]{3,2,1,0:T(8,128)S(1)}, u32[]{:S(2)}, u32[]{:S(2)}) %collective-permute-start) | collective-permute-done | bytes 786464 | tf_op jit(solution)/shard_map/ppermute | solution.py:204
  21.4 0.0 copy-start.1
  21.4 0.1 add.6
  21.5 31.9 %all_to_all.30.pieces_ref = f32[64,3,8,128]{3,2,1,0:T(8,128)S(1)} all-to-all(f32[64,3,8,128]{3,2,1,0:T(8,128)S(1)} %add.6), channel_id=1, replica_groups={{0,16,32,48,64,80,96,112,128,144,160,176,192,208,224,240,256,272,288,30..., dimensions={0} | all-to-all | bytes 1572864 | tf_op jit(solution)/shard_map/all_to_all | solution.py:206
  53.4 0.0 copy-done.1
  53.4 0.0 copy-start.2
  53.4 0.7 piece.1
  54.1 13.5 %all_to_all.31.parts_ref = f32[8,8,256]{2,1,0:T(8,128)S(1)} all-to-all(f32[8,8,256]{2,1,0:T(8,128)S(1)} %broadcast_in_dim.6), channel_id=1, replica_groups=mesh['dp'=128,'tensor'=8] {'tensor'}, dimensions={0} | all-to-all | bytes 131072 | tf_op jit(solution)/shard_map/all_to_all | solution.py:213
  67.6 0.5 image.1
  68.0 20.2 %all_to_all.32 = f32[64,1,640]{2,1,0:T(1,128)S(1)} all-to-all(f32[64,1,640]{2,1,0:T(1,128)S(1)} %bitcast.9), channel_id=1, replica_groups={{0,16,32,48,64,80,96,112,128,144,160,176,192,208,224,240,256,272,288,30..., dimensions={0} | all-to-all | bytes 327680 | tf_op jit(solution)/shard_map/all_to_all | solution.py:219
  88.2 0.1 reduce_sum.9
  88.3 5.5 %collective-permute-start.1 = (f32[640]{0:T(1024)S(1)}, f32[640]{0:T(1024)S(1)}, u32[]{:S(2)}, u32[]{:S(2)}) collective-permute-start(f32[640]{0:T(1024)S(1)} %reduce_sum.9), channel_id=1, source_target_pairs={{0,8},{8,0},{16,24},{24,16},{32,40},{40,32},{48,56},{56,48},{64,72... | collective-permute-start | bytes 7688 | tf_op jit(solution)/shard_map/ppermute | solution.py:221
  93.9 0.8 collective-permute-done.1
  94.7 0.1 broadcast_in_dim.7
  94.8 15.7 %all_to_all.33 = f32[64,1,640]{2,1,0:T(1,128)S(1)} all-to-all(f32[64,1,640]{2,1,0:T(1,128)S(1)} %broadcast_in_dim.7), channel_id=1, replica_groups={{0,16,32,48,64,80,96,112,128,144,160,176,192,208,224,240,256,272,288,30..., dimensions={0} | all-to-all | bytes 327680 | tf_op jit(solution)/shard_map/all_to_all | solution.py:222
  110.4 9.5 %first.1 = (f32[3,64,128]{2,1,0:T(8,128)S(1)}, f32[3,24,128]{2,1,0:T(8,128)S(1)}) custom-call(f32[320,128]{1,0:T(8,128)S(1)} %bitcast.8), custom_call_target="tpu_custom_call" | custom-call | tf_op jit(solution)/shard_map/first/pallas_call | solution.py:225
  119.9 12.2 %all_to_all.34.grams_ref = f32[8,3,24,128]{3,2,1,0:T(8,128)S(1)} all-to-all(f32[8,3,24,128]{3,2,1,0:T(8,128)S(1)} %broadcast_in_dim.8), channel_id=1, replica_groups=mesh['dp'=128,'tensor'=8] {'tensor'}, dimensions={0} | all-to-all | bytes 589824 | tf_op jit(solution)/shard_map/all_to_all | solution.py:228
  132.1 0.0 copy-done.2
  132.1 10.2 %second.1 = (f32[3,64,128]{2,1,0:T(8,128)}, f32[3,64]{1,0:T(4,128)}, f32[2,64]{1,0:T(2,128)}) custom-call(s32[3]{0:T(128)S(1)} %copy-done.2, s32[1]{0:T(128)} %bitcast.4.index_ref, f32[3,64,128]{2,1,0:T(8,128)S(1)} %get-tuple-element.19.image_ref, f32[8,3,24,128]{3,2,1,0:T(8,128)S(1)} %all_to_all.34.grams_ref), custom_call_target="tpu_custom_call" | custom-call | tf_op jit(solution)/shard_map/second/pallas_call | solution.py:231
  (3 shorter events, 0.0 us)
Async XLA Ops:
  0.6 1.4 copy-start
  3.5 17.9 %collective-permute-start = (f32[64,3,8,128]{3,2,1,0:T(8,128)S(1)}, f32[64,3,8,128]{3,2,1,0:T(8,128)S(1)}, u32[]{:S(2)}, u32[]{:S(2)}) collective-permute-start(f32[64,3,8,128]{3,2,1,0:T(8,128)S(1)} %get-tuple-element.15), channel_id=1, source_target_pairs={{0,8},{8,0},{16,24},{24,16},{32,40},{40,32},{48,56},{56,48},{64,72... | collective-permute-start | bytes 2359304 | tf_op jit(solution)/shard_map/ppermute | solution.py:204
  21.4 32.0 %copy-start.1 = (f32[3,128,64]{1,2,0:T(8,128)S(1)}, f32[3,128,64]{1,2,0:T(8,128)}, u32[]{:S(2)}) copy-start(f32[3,128,64]{1,2,0:T(8,128)} %param.4) | copy-start | bytes 294916
  53.4 78.8 %copy-start.2 = (s32[3]{0:T(128)S(1)}, s32[3]{0:T(128)}, u32[]{:S(2)}) copy-start(s32[3]{0:T(128)} %owner_ref.1) | copy-start | bytes 40
  88.3 6.3 %collective-permute-start.1 = (f32[640]{0:T(1024)S(1)}, f32[640]{0:T(1024)S(1)}, u32[]{:S(2)}, u32[]{:S(2)}) collective-permute-start(f32[640]{0:T(1024)S(1)} %reduce_sum.9), channel_id=1, source_target_pairs={{0,8},{8,0},{16,24},{24,16},{32,40},{40,32},{48,56},{56,48},{64,72... | collective-permute-start | bytes 7688 | tf_op jit(solution)/shard_map/ppermute | solution.py:221
